TPU v7x, 32 devices: a whole 2x2x4 slice. The times are simulated.
32 devices in a mesh: dp: 8 (over z, y), tensor: 4 (over x, core).
Axes of the slice: x: 2, y: 2, z: 4, core: 2. Of those that a mesh axis runs over, the one named last changes fastest.
Arguments:
- inputs: bfloat16 [8192, 1024], P(('dp', 'tensor')), may hold values from -6 to 6
- doc_ids: int32 [8, 1024], P('dp'), may hold values from 0 to 1, as said below
- w_qkv: bfloat16 [3, 1024, 1024], P(None, None, 'tensor'), may hold values from -0.1875 to 0.1875
- w_out: bfloat16 [1024, 1024], P('tensor'), may hold values from -0.1875 to 0.1875
- w_up: bfloat16 [1024, 4096], P(None, 'tensor'), may hold values from -0.1875 to 0.1875
- w_down: bfloat16 [4096, 1024], P('tensor'), may hold values from -0.09375 to 0.09375
- norm_gain: float32 [4, 1024], replicated, may hold values from 0.25 to 1.75
- norm_bias: float32 [4, 1024], replicated, may hold values from -1.5 to 1.5
- out_grad: bfloat16 [8192, 1024], P(('dp', 'tensor')), may hold values from -6 to 6
Outputs:
- output: bfloat16 [8192, 1024], P(('dp', 'tensor'))
- grad_inputs: bfloat16 [8192, 1024], P(('dp', 'tensor'))
- grad_qkv: float32 [3, 1024, 1024], P(None, None, 'tensor')
- grad_wout: float32 [1024, 1024], P('tensor')
- grad_up: float32 [1024, 4096], P(None, 'tensor')
- grad_down: float32 [4096, 1024], P('tensor')
- grad_gain: float32 [4, 1024], replicated
- grad_bias: float32 [4, 1024], replicated
Inputs may be any that keep to these rules, and one draw needn't show every extreme that they name: `doc_ids`: in each group either every token is in document 0, or token i is in document i // 512; exactly half of the groups are of the first kind.
All inputs are finite; a program needn't handle non-finite values.
Results may differ from a plain program's by a relative error of at most 0.015.
Values may be sent and summed in bfloat16 or wider, within the bound.
No kernel may reach another device: no remote copies, remote signals or barrier semaphores. Data moves between devices by JAX's collectives and lax.ppermute only.
A program may use at most 128 MiB of HBM per device.

v0:
```python
import jax
import jax.numpy as jnp
from jax import lax
from jax.sharding import PartitionSpec as P

HEAD_DIM = 64
eps = 1e-05


def rope_tables(doc_row):
    length_all = doc_row.shape[0]
    places = jnp.arange(length_all, dtype=jnp.int32)
    earlier = jnp.concatenate([doc_row[:1], doc_row[:-1]])
    starting = jnp.logical_and(doc_row != earlier, places > 0)
    first_pos = lax.cummax(jnp.where(starting, places, 0), axis=0)
    place = (places - first_pos).astype(jnp.float32)
    half = HEAD_DIM // 2
    freqs = 10000.0 ** (-jnp.arange(half, dtype=jnp.float32) / half)
    angles = place[:, None] * freqs[None, :]
    return (jnp.cos(angles), jnp.sin(angles))


def rotate(values_in, cosine, sine_table):
    half = values_in.shape[-1] // 2
    first = values_in[..., :half]
    second = values_in[..., half:]
    cos_wide = cosine[:, None, :]
    sin_wide = sine_table[:, None, :]
    return jnp.concatenate(
        [first * cos_wide - second * sin_wide, second * cos_wide + first * sin_wide], axis=-1
    )


def rotate_back(grad_in, cosine, sine_table):
    half = grad_in.shape[-1] // 2
    first = grad_in[..., :half]
    second = grad_in[..., half:]
    cos_wide = cosine[:, None, :]
    sin_wide = sine_table[:, None, :]
    return jnp.concatenate(
        [first * cos_wide + second * sin_wide, second * cos_wide - first * sin_wide], axis=-1
    )


def block_mask(doc_row, offset, block_rows):
    places = jnp.arange(doc_row.shape[0], dtype=jnp.int32)
    query_pos = offset + jnp.arange(block_rows, dtype=jnp.int32)
    query_doc = lax.dynamic_slice_in_dim(doc_row, offset, block_rows, 0)
    return jnp.logical_and(
        places[None, :] <= query_pos[:, None], doc_row[None, :] == query_doc[:, None]
    )


def norm_forward(values_in, gain, bias):
    center = values_in - jnp.mean(values_in, axis=-1, keepdims=True)
    spread = jnp.mean(center * center, axis=-1, keepdims=True)
    scale_inv = lax.rsqrt(spread + eps)
    unit = center * scale_inv
    return (unit * gain + bias, unit, scale_inv)


def norm_backward(upstream, unit, scale_inv, gain):
    scaled = upstream * gain
    result = scale_inv * (
        scaled
        - jnp.mean(scaled, axis=-1, keepdims=True)
        - unit * jnp.mean(scaled * unit, axis=-1, keepdims=True)
    )
    return (result, jnp.sum(upstream * unit, axis=0), jnp.sum(upstream, axis=0))


def gelu_exact(values_in):
    return 0.5 * values_in * (1.0 + jax.scipy.special.erf(values_in * 0.7071067811865476))


def gelu_slope(values_in):
    return (
        0.5 * (1.0 + jax.scipy.special.erf(values_in * 0.7071067811865476))
        + values_in * jnp.exp(-0.5 * values_in * values_in) * 0.3989422804014327
    )


def gather_rows(values_in):
    return lax.all_gather(values_in, "tensor", axis=0, tiled=True)


def row_sums(term, own_rows):
    return lax.psum_scatter(
        term(jnp.int32(0), own_rows * lax.axis_size("tensor")),
        "tensor",
        scatter_dimension=0,
        tiled=True,
    )


def attention_forward(query_rot, key_rot, value_all, doc_row):
    length_all = query_rot.shape[0]
    block_rows = min(512, length_all)
    scaling = HEAD_DIM ** (-0.5)

    def attend(offset):
        query_block = lax.dynamic_slice_in_dim(query_rot, offset, block_rows, 0)
        scores = (
            jnp.einsum("qhd,khd->hqk", query_block, key_rot, preferred_element_type=jnp.float32)
            * scaling
        )
        scores = jnp.where(block_mask(doc_row, offset, block_rows)[None], scores, -1e30)
        row_max = jnp.max(scores, axis=-1, keepdims=True)
        exp_scores = jnp.exp(scores - row_max)
        row_total = jnp.sum(exp_scores, axis=-1, keepdims=True)
        weights = (exp_scores / row_total).astype(jnp.bfloat16)
        attended = jnp.einsum(
            "hqk,khd->qhd", weights, value_all, preferred_element_type=jnp.float32
        )
        return (attended.astype(jnp.bfloat16), (row_max + jnp.log(row_total))[..., 0])

    offsets = jnp.arange(length_all // block_rows, dtype=jnp.int32) * block_rows
    head_out, log_total = lax.map(attend, offsets)
    return (head_out.reshape(length_all, -1), log_total)


def attention_backward(query_rot, key_rot, value_all, doc_row, grad_heads, log_total):
    length_all = query_rot.shape[0]
    block_rows = min(512, length_all)
    scaling = HEAD_DIM ** (-0.5)

    def step_back(running, item):
        offset, total_block = item
        query_block = lax.dynamic_slice_in_dim(query_rot, offset, block_rows, 0)
        grad_block = lax.dynamic_slice_in_dim(grad_heads, offset, block_rows, 0)
        scores = (
            jnp.einsum("qhd,khd->hqk", query_block, key_rot, preferred_element_type=jnp.float32)
            * scaling
        )
        scores = jnp.where(block_mask(doc_row, offset, block_rows)[None], scores, -1e30)
        probs = jnp.exp(scores - total_block[..., None])
        grad_probs = jnp.einsum(
            "qhd,khd->hqk", grad_block, value_all, preferred_element_type=jnp.float32
        )
        delta = jnp.sum(probs * grad_probs, axis=-1, keepdims=True)
        grad_scores = (probs * (grad_probs - delta) * scaling).astype(jnp.bfloat16)
        grad_query = jnp.einsum(
            "hqk,khd->qhd", grad_scores, key_rot, preferred_element_type=jnp.float32
        )
        grad_key = running[0] + jnp.einsum(
            "hqk,qhd->khd", grad_scores, query_block, preferred_element_type=jnp.float32
        )
        grad_value = running[1] + jnp.einsum(
            "hqk,qhd->khd",
            probs.astype(jnp.bfloat16),
            grad_block,
            preferred_element_type=jnp.float32,
        )
        return ((grad_key, grad_value), grad_query)

    offsets = jnp.arange(length_all // block_rows, dtype=jnp.int32) * block_rows
    zeros_kv = jnp.zeros(key_rot.shape, jnp.float32)
    (grad_key, grad_value), grad_query = lax.scan(
        step_back, (zeros_kv, zeros_kv), (offsets, log_total)
    )
    return (grad_query.reshape(key_rot.shape), grad_key, grad_value)


def per_device(inputs, doc_ids, w_qkv, w_out, w_up, w_down, norm_gain, norm_bias, out_grad):
    own_rows = inputs.shape[0]
    doc_row = doc_ids[0]
    length_all = doc_row.shape[0]
    cosine, sine_table = rope_tables(doc_row)
    local_heads = w_qkv.shape[2] // HEAD_DIM
    shaped = (length_all, local_heads, HEAD_DIM)
    rows_f32 = inputs.astype(jnp.float32)
    normed, unit0, inv0 = norm_forward(rows_f32, norm_gain[0], norm_bias[0])
    gathered = gather_rows(normed.astype(jnp.bfloat16))
    projected = jnp.einsum("td,jde->jte", gathered, w_qkv, preferred_element_type=jnp.float32)
    query_rot = rotate(projected[0].reshape(shaped), cosine, sine_table).astype(jnp.bfloat16)
    key_rot = rotate(projected[1].reshape(shaped), cosine, sine_table).astype(jnp.bfloat16)
    value_all = projected[2].reshape(shaped).astype(jnp.bfloat16)
    head_flat, log_total = attention_forward(query_rot, key_rot, value_all, doc_row)

    def out_term(offset, amount):
        return jnp.dot(head_flat, w_out, preferred_element_type=jnp.float32)

    attended = row_sums(out_term, own_rows)
    attn_normed, unit1, inv1 = norm_forward(attended, norm_gain[1], norm_bias[1])
    middle = rows_f32 + attn_normed
    normed2, unit2, inv2 = norm_forward(middle, norm_gain[2], norm_bias[2])
    normed2_low = normed2.astype(jnp.bfloat16)
    gathered2 = gather_rows(normed2_low)
    hidden = jnp.dot(gathered2, w_up, preferred_element_type=jnp.float32)
    activated = gelu_exact(hidden).astype(jnp.bfloat16)

    def down_term(offset, amount):
        return jnp.dot(activated, w_down, preferred_element_type=jnp.float32)

    mixed = row_sums(down_term, own_rows)
    mixed_normed, unit3, inv3 = norm_forward(mixed, norm_gain[3], norm_bias[3])
    output = (middle + mixed_normed).astype(jnp.bfloat16)
    grad_out = out_grad.astype(jnp.float32)
    grad_mixed, gain3, bias3 = norm_backward(grad_out, unit3, inv3, norm_gain[3])
    grad_mixed_low = grad_mixed.astype(jnp.bfloat16)
    grad_mixed_all = gather_rows(grad_mixed_low)
    grad_down = jnp.einsum(
        "tf,td->fd", activated, grad_mixed_all, preferred_element_type=jnp.float32
    )
    grad_act = jnp.einsum("td,fd->tf", grad_mixed_all, w_down, preferred_element_type=jnp.float32)
    grad_hidden = (grad_act * gelu_slope(hidden)).astype(jnp.bfloat16)
    grad_up = jnp.einsum("td,tf->df", gathered2, grad_hidden, preferred_element_type=jnp.float32)

    def up_term(offset, amount):
        return jnp.einsum("tf,df->td", grad_hidden, w_up, preferred_element_type=jnp.float32)

    grad_normed2 = row_sums(up_term, own_rows)
    back2, gain2, bias2 = norm_backward(grad_normed2, unit2, inv2, norm_gain[2])
    grad_middle = grad_out + back2
    grad_attended, gain1, bias1 = norm_backward(grad_middle, unit1, inv1, norm_gain[1])
    grad_attended_all = gather_rows(grad_attended.astype(jnp.bfloat16))
    grad_wout = jnp.einsum(
        "te,td->ed", head_flat, grad_attended_all, preferred_element_type=jnp.float32
    )
    grad_heads = (
        jnp.einsum("td,ed->te", grad_attended_all, w_out, preferred_element_type=jnp.float32)
        .astype(jnp.bfloat16)
        .reshape(shaped)
    )
    grad_query, grad_key, grad_value = attention_backward(
        query_rot, key_rot, value_all, doc_row, grad_heads, log_total
    )
    flat_width = local_heads * HEAD_DIM
    grad_proj = jnp.stack(
        [
            rotate_back(grad_query, cosine, sine_table).reshape(length_all, flat_width),
            rotate_back(grad_key, cosine, sine_table).reshape(length_all, flat_width),
            grad_value.reshape(length_all, flat_width),
        ],
        axis=0,
    ).astype(jnp.bfloat16)
    grad_qkv = jnp.einsum("td,jte->jde", gathered, grad_proj, preferred_element_type=jnp.float32)

    def qkv_term(offset, amount):
        return jnp.einsum("jte,jde->td", grad_proj, w_qkv, preferred_element_type=jnp.float32)

    grad_normed = row_sums(qkv_term, own_rows)
    back0, gain0, bias0 = norm_backward(grad_normed, unit0, inv0, norm_gain[0])
    grad_inputs = (grad_middle + back0).astype(jnp.bfloat16)
    grad_qkv, grad_wout, grad_up, grad_down = lax.psum(
        (grad_qkv, grad_wout, grad_up, grad_down), "dp"
    )
    grad_gain, grad_bias = lax.psum(
        (
            jnp.stack([gain0, gain1, gain2, gain3], axis=0),
            jnp.stack([bias0, bias1, bias2, bias3], axis=0),
        ),
        ("dp", "tensor"),
    )
    return (output, grad_inputs, grad_qkv, grad_wout, grad_up, grad_down, grad_gain, grad_bias)


def solution(mesh):
    return jax.shard_map(
        per_device,
        mesh=mesh,
        in_specs=(
            P(("dp", "tensor"), None),
            P("dp", None),
            P(None, None, "tensor"),
            P("tensor", None),
            P(None, "tensor"),
            P("tensor", None),
            P(),
            P(),
            P(("dp", "tensor"), None),
        ),
        out_specs=(
            P(("dp", "tensor"), None),
            P(("dp", "tensor"), None),
            P(None, None, "tensor"),
            P("tensor", None),
            P(None, "tensor"),
            P("tensor", None),
            P(),
            P(),
        ),
        check_vma=False,
    )
```

profile of v0, /device:TPU:0, one launch (start us, length us, event | category | flops | bytes accessed | tf_op | source)
XLA Modules:
  0.0 931.0 jit_solution(6733210452404550416)
XLA Ops:
  17.7 21.6 %all-gather.5.cloned.1.call-done = bf16[1024,1024]{1,0:T(8,128)(2,1)} async-done(((bf16[256,1024]{1,0:T(8,128)(2,1)}), bf16[1024,1024]{1,0:T(8,128)(2,1)}) %all-gather.5.cloned.1.call-update) | async-done | bytes 2097168 | tf_op jit(solution)/shard_map/all_gather | solution.py:84
  39.3 3.9 fusion.90
  44.7 25.8 %while.27 = (s32[]{:T(128)}, bf16[2,512,4,64]{1,3,2,0:T(8,128)(2,1)}, f32[2,4,512]{2,1,0:T(4,128)S(1)}, s32[2]{0:T(128)S(1)}, s32[1,1024]{1,0:T(1,128)S(1)}, /*i...) while((s32[]{:T(128)}, ...), condition=%wide.region_7.8_spmd, body=%wide.region_4.7_spmd.sunk | while | flops 563739136 | bytes 33110264 | solution.py:118
  73.0 3.8 fusion.130
  76.8 44.7 %reduce-scatter.5.cloned.1.call-done = f32[256,1024]{1,0:T(8,128)} async-done(((f32[1024,1024]{1,0:T(8,128)}), f32[256,1024]{1,0:T(8,128)}) %reduce-scatter.5.cloned.1.call-update) | async-done | bytes 1048592 | tf_op jit(solution)/shard_map/reduce_scatter | solution.py:88
  128.7 22.2 %all-gather.7.cloned.1.call-done = bf16[1024,1024]{1,0:T(8,128)(2,1)} async-done(((bf16[256,1024]{1,0:T(8,128)(2,1)}), bf16[1024,1024]{1,0:T(8,128)(2,1)}) %all-gather.7.cloned.1.call-update) | async-done | bytes 2097168 | tf_op jit(solution)/shard_map/all_gather | solution.py:84
  150.9 5.8 multiply_convert_fusion.1
  158.1 4.4 fusion.131
  162.5 44.7 %reduce-scatter.7.cloned.1.call-done = f32[256,1024]{1,0:T(8,128)} async-done(((f32[1024,1024]{1,0:T(8,128)}), f32[256,1024]{1,0:T(8,128)}) %reduce-scatter.7.cloned.1.call-update) | async-done | bytes 1048592 | tf_op jit(solution)/shard_map/reduce_scatter | solution.py:88
  215.2 22.7 %all-gather.9.cloned.1.call-done = bf16[1024,1024]{1,0:T(8,128)(2,1)} async-done(((bf16[256,1024]{1,0:T(8,128)(2,1)}), bf16[1024,1024]{1,0:T(8,128)(2,1)}) %all-gather.9.cloned.1.call-update) | async-done | bytes 2097168 | tf_op jit(solution)/shard_map/all_gather | solution.py:84
  237.9 6.2 fusion.85
  245.4 4.4 fusion.132
  249.9 44.7 %reduce-scatter.9.cloned.1.call-done = f32[256,1024]{1,0:T(8,128)} async-done(((f32[1024,1024]{1,0:T(8,128)}), f32[256,1024]{1,0:T(8,128)}) %reduce-scatter.9.cloned.1.call-update) | async-done | bytes 1048592 | tf_op jit(solution)/shard_map/reduce_scatter | solution.py:88
  300.9 22.6 %all-gather.11.cloned.1.call-done = bf16[1024,1024]{1,0:T(8,128)(2,1)} async-done(((bf16[256,1024]{1,0:T(8,128)(2,1)}), bf16[1024,1024]{1,0:T(8,128)(2,1)}) %all-gather.11.cloned.1.call-update) | async-done | bytes 2097168 | tf_op jit(solution)/shard_map/all_gather | solution.py:84
  326.0 130.7 %while.28 = (s32[]{:T(128)}, f32[1024,4,64]{0,2,1:T(8,128)}, f32[1024,4,64]{0,2,1:T(8,128)}, f32[2,512,4,64]{1,0,3,2:T(2,128)}, s32[2]{0:T(128)S(1)}, /*index=5*...) while((s32[]{:T(128)}, f32[1024,4,64]{0,2,1:T(8,128)}, ...), condition=%wide.region_25.26_spmd.clone, body=%wide.region_23.25_spmd.clone.sunk | while | flops 1399331328 | bytes 129562944 | solution.py:158
  335.6 4.6 fusion.199
  340.2 17.1 %fusion.204 = f32[1,512,4,64]{1,3,2,0:T(8,128)S(1)} fusion(bf16[1024,4,64]{0,2,1:T(8,128)(2,1)S(1)} %get-tuple-element.485, f32[4,512,1024]{2,1,0:T(8,128)} %fusion.199, f32[4,512,1024]{2,1,0:T(8,128)} %copy-done.2, f32[4,512]{1,0:T(4,128)S(1)} %dynamic-slice_bitcast_fusion.2, pred[512,1024]{1,0:T(8,128)(4,1)S(1)} %fusion.201), kind=kOutput, calls=%fused_computation.42.clone.1 | convolution fusion | flops 291507200 | bytes 18358272 | tf_op jit(solution)/shard_map/while/body/eval_jaxpr/hqk,khd->qhd/dot_general | solution.py:142
  357.4 23.1 %fusion.202 = f32[1024,4,64]{0,2,1:T(8,128)} fusion(f32[4,512,1024]{2,1,0:T(8,128)} %fusion.199, f32[4,512,1024]{2,1,0:T(8,128)} %copy-done.2, f32[4,512]{1,0:T(4,128)S(1)} %dynamic-slice_bitcast_fusion.2, pred[512,1024]{1,0:T(8,128)(4,1)S(1)} %fusion.201, f32[1024,4,64]{0,2,1:T(8,128)} %get-tuple-element.463, pred[]{:T(512)S(6)} %compare.3, ...), kind=kOutput, calls=%fused_computation.40.clone.1 | convolution fusion | flops 292031488 | bytes 36978692 | tf_op jit(solution)/shard_map/while/body/eval_jaxpr/hqk,qhd->khd/dot_general | solution.py:145
  381.0 10.3 %dynamic_update_slice.20 = f32[2,512,4,64]{1,0,3,2:T(2,128)} dynamic-update-slice(f32[2,512,4,64]{1,0,3,2:T(2,128)} %get-tuple-element.465, f32[1,512,4,64]{1,0,3,2:T(1,128)S(1)} %copy.61, s32[]{:T(128)S(6)} %copy.78, s32[]{:T(128)} %constant.76.clone.1..sunk.1, s32[]{:T(128)} %constant.76.clone.1..sunk.1, s32[]{:T(128)} %constant.76.clone.1..sunk.1) | dynamic-update-slice | bytes 1048580 | tf_op jit(solution)/shard_map/while/body/jit(dynamic_update_index_in_dim)/dynamic_update_slice | solution.py:158
  400.7 4.6 fusion.199
  405.3 17.1 %fusion.204 = f32[1,512,4,64]{1,3,2,0:T(8,128)S(1)} fusion(bf16[1024,4,64]{0,2,1:T(8,128)(2,1)S(1)} %get-tuple-element.485, f32[4,512,1024]{2,1,0:T(8,128)} %fusion.199, f32[4,512,1024]{2,1,0:T(8,128)} %copy-done.2, f32[4,512]{1,0:T(4,128)S(1)} %dynamic-slice_bitcast_fusion.2, pred[512,1024]{1,0:T(8,128)(4,1)S(1)} %fusion.201), kind=kOutput, calls=%fused_computation.42.clone.1 | convolution fusion | flops 291507200 | bytes 18358272 | tf_op jit(solution)/shard_map/while/body/eval_jaxpr/hqk,khd->qhd/dot_general | solution.py:142
  422.5 23.2 %fusion.202 = f32[1024,4,64]{0,2,1:T(8,128)} fusion(f32[4,512,1024]{2,1,0:T(8,128)} %fusion.199, f32[4,512,1024]{2,1,0:T(8,128)} %copy-done.2, f32[4,512]{1,0:T(4,128)S(1)} %dynamic-slice_bitcast_fusion.2, pred[512,1024]{1,0:T(8,128)(4,1)S(1)} %fusion.201, f32[1024,4,64]{0,2,1:T(8,128)} %get-tuple-element.463, pred[]{:T(512)S(6)} %compare.3, ...), kind=kOutput, calls=%fused_computation.40.clone.1 | convolution fusion | flops 292031488 | bytes 36978692 | tf_op jit(solution)/shard_map/while/body/eval_jaxpr/hqk,qhd->khd/dot_general | solution.py:145
  446.2 10.3 %dynamic_update_slice.20 = f32[2,512,4,64]{1,0,3,2:T(2,128)} dynamic-update-slice(f32[2,512,4,64]{1,0,3,2:T(2,128)} %get-tuple-element.465, f32[1,512,4,64]{1,0,3,2:T(1,128)S(1)} %copy.61, s32[]{:T(128)S(6)} %copy.78, s32[]{:T(128)} %constant.76.clone.1..sunk.1, s32[]{:T(128)} %constant.76.clone.1..sunk.1, s32[]{:T(128)} %constant.76.clone.1..sunk.1) | dynamic-update-slice | bytes 1048580 | tf_op jit(solution)/shard_map/while/body/jit(dynamic_update_index_in_dim)/dynamic_update_slice | solution.py:158
  461.3 5.4 convolution_bitcast_fusion
  468.3 6.0 fusion.135
  474.4 4.4 fusion.134
  480.6 3.5 fusion.93
  484.2 27.3 %reduce-scatter.11.cloned.1.call-done = f32[256,1024]{1,0:T(8,128)} async-done(((f32[1024,1024]{1,0:T(8,128)}), f32[256,1024]{1,0:T(8,128)}) %reduce-scatter.11.cloned.1.call-update) | async-done | bytes 1048592 | tf_op jit(solution)/shard_map/reduce_scatter | solution.py:88
  513.3 43.8 %all-reduce = (f32[4,1024]{1,0:T(4,128)}, f32[4,1024]{1,0:T(4,128)}) all-reduce(f32[4,1024]{1,0:T(4,128)S(1)} %pad_maximum_fusion.7, f32[4,1024]{1,0:T(4,128)S(1)} %pad_maximum_fusion.8), channel_id=1, replica_groups=mesh['dp'=8,'tensor'=4] {'dp','tensor'}, use_global_device_ids=true, to_apply=%region_37.38 | all-reduce | flops 8192 | bytes 65536 | tf_op jit(solution)/shard_map/psum | solution.py:248
  559.5 353.0 %all-reduce.4.cloned.1.call-done = (f32[3,1024,256]{1,2,0:T(8,128)}, f32[256,1024]{1,0:T(8,128)}, f32[1024,1024]{1,0:T(8,128)}, f32[1024,1024]{1,0:T(8,128)}) async-done(((f32[3,1024,256]{1,2,0:T(8,128)}, f32[256,1024]{1,0:T(8,128)}, f32[1024,1024]{1,0:T(8,128)}, f32[1024,1024]{1,0:T(8,128)}), (f32[3,1024,256]{1,2,0:T(8,128)}, f32[256,1024]{1,0:T(8,128)}, f32[1024,1024]{1,0:T(8,128)}, ...) | async-done | bytes 12582928 | tf_op jit(solution)/shard_map/psum | solution.py:245
  912.6 3.6 copy.30
  917.2 4.9 copy.91
  (214 shorter events, 93.6 us)
Async XLA Ops:
  7.2 143.8 %copy-start = (bf16[1024,1024]{1,0:T(8,128)(2,1)S(1)}, bf16[1024,1024]{1,0:T(8,128)(2,1)}, u32[]{:S(2)}) copy-start(bf16[1024,1024]{1,0:T(8,128)(2,1)} %param.17) | copy-start | bytes 6291460
  7.2 32.1 %all-gather.5.cloned.1.call-start = ((), (), s32[]{:S(2)}) async-start(), calls=%async_computation.4 | async-start | bytes 2621440 | tf_op jit(solution)/shard_map/all_gather | solution.py:84
  8.6 6.5 copy-start.31
  9.9 6.9 copy-start.33
  10.8 6.3 copy-start.29
  13.8 107.7 %reduce-scatter.5.cloned.1.call-start = ((), (), s32[]{:S(2)}) async-start(), calls=%async_computation.5 | async-start | bytes 5242880 | tf_op jit(solution)/shard_map/reduce_scatter | solution.py:88
  17.7 25.7 %copy-start.15 = (f32[1024,32]{0,1:T(8,128)}, f32[1024,32]{0,1:T(8,128)S(1)}, u32[]{:S(2)}) copy-start(f32[1024,32]{0,1:T(8,128)S(1)} %get-tuple-element.273) | copy-start | bytes 393220
  17.7 25.7 %copy-start.17 = (f32[1024,32]{0,1:T(8,128)}, f32[1024,32]{0,1:T(8,128)S(1)}, u32[]{:S(2)}) copy-start(f32[1024,32]{0,1:T(8,128)S(1)} %get-tuple-element.274) | copy-start | bytes 393220
  76.8 74.1 %all-gather.7.cloned.1.call-start = ((), (), s32[]{:S(2)}) async-start(), calls=%async_computation.6 | async-start | bytes 2621440 | tf_op jit(solution)/shard_map/all_gather | solution.py:84
  128.2 79.0 %reduce-scatter.7.cloned.1.call-start = ((), (), s32[]{:S(2)}) async-start(), calls=%async_computation.7 | async-start | bytes 5242880 | tf_op jit(solution)/shard_map/reduce_scatter | solution.py:88
  150.9 7.2 copy-start.35
  162.5 75.4 %all-gather.9.cloned.1.call-start = ((), (), s32[]{:S(2)}) async-start(), calls=%async_computation.8 | async-start | bytes 2621440 | tf_op jit(solution)/shard_map/all_gather | solution.py:84
  215.2 79.5 %reduce-scatter.9.cloned.1.call-start = ((), (), s32[]{:S(2)}) async-start(), calls=%async_computation.9 | async-start | bytes 5242880 | tf_op jit(solution)/shard_map/reduce_scatter | solution.py:88
  249.9 44.8 %copy-start.4 = (f32[256,1024]{1,0:T(8,128)S(1)}, f32[256,1024]{1,0:T(8,128)}, u32[]{:S(2)}) copy-start(f32[256,1024]{1,0:T(8,128)} %copy-done.3) | copy-start | bytes 3145732
  249.9 46.5 %copy-start.5 = (f32[256,1024]{1,0:T(8,128)S(1)}, f32[256,1024]{1,0:T(8,128)}, u32[]{:S(2)}) copy-start(f32[256,1024]{1,0:T(8,128)} %reduce-scatter.5.cloned.1.call-done) | copy-start | bytes 3145732
  249.9 73.7 %all-gather.11.cloned.1.call-start = ((), (), s32[]{:S(2)}) async-start(), calls=%async_computation.10 | async-start | bytes 2621440 | tf_op jit(solution)/shard_map/all_gather | solution.py:84
  299.7 26.3 %copy-start.6 = (bf16[1024,4,64]{0,2,1:T(8,128)(2,1)S(1)}, bf16[1024,4,64]{0,2,1:T(8,128)(2,1)}, u32[]{:S(2)}) copy-start(bf16[1024,4,64]{0,2,1:T(8,128)(2,1)} %get-tuple-element.521) | copy-start | bytes 1572868
  300.9 210.6 %reduce-scatter.11.cloned.1.call-start = ((), (), s32[]{:S(2)}) async-start(), calls=%async_computation.11 | async-start | bytes 5242880 | tf_op jit(solution)/shard_map/reduce_scatter | solution.py:88
  326.0 132.8 %copy-start.16 = (f32[1024,32]{0,1:T(8,128)S(1)}, f32[1024,32]{0,1:T(8,128)}, u32[]{:S(2)}) copy-start(f32[1024,32]{0,1:T(8,128)} %copy-done.15) | copy-start | bytes 393220
  326.0 132.8 %copy-start.18 = (f32[1024,32]{0,1:T(8,128)S(1)}, f32[1024,32]{0,1:T(8,128)}, u32[]{:S(2)}) copy-start(f32[1024,32]{0,1:T(8,128)} %copy-done.17) | copy-start | bytes 393220
  466.8 445.8 %all-reduce.4.cloned.1.call-start = ((), (), s32[]{:S(2)}) async-start(), calls=%async_computation.12 | async-start | bytes 25165824 | tf_op jit(solution)/shard_map/psum | solution.py:245
  468.3 6.1 copy-start.37
  468.3 6.1 copy-start.41
  474.4 6.2 copy-start.26
  474.4 6.2 copy-start.28
  474.4 6.2 copy-start.36
  484.1 27.4 %copy-start.7 = (bf16[256,1024]{1,0:T(8,128)(2,1)S(1)}, bf16[256,1024]{1,0:T(8,128)(2,1)}, u32[]{:S(2)}) copy-start(bf16[256,1024]{1,0:T(8,128)(2,1)} %param.13) | copy-start | bytes 1572868
  484.1 27.4 %copy-start.30 = (f32[1,1024]{1,0:T(1,128)S(1)}, f32[1,1024]{1,0:T(1,128)}, u32[]{:S(2)}) copy-start(f32[1,1024]{1,0:T(1,128)} %copy-done.29) | copy-start | bytes 12292
  484.1 27.4 %copy-start.32 = (f32[256]{0:T(256)S(1)}, f32[256]{0:T(256)}, u32[]{:S(2)}) copy-start(f32[256]{0:T(256)} %copy-done.31) | copy-start | bytes 3076
  484.1 27.4 %copy-start.34 = (f32[256]{0:T(256)S(1)}, f32[256]{0:T(256)}, u32[]{:S(2)}) copy-start(f32[256]{0:T(256)} %copy-done.33) | copy-start | bytes 3076
  484.1 73.0 %copy-start.9 = (f32[256,1024]{1,0:T(8,128)S(1)}, f32[256,1024]{1,0:T(8,128)}, u32[]{:S(2)}) copy-start(f32[256,1024]{1,0:T(8,128)} %copy-done.8) | copy-start | bytes 3145732
  917.2 7.0 copy-start.1
  (24 other events, 56.8 us)
Sparse Core Ops, SparseCore 0:
  14.0 25.2 all-gather.4
  76.9 44.5 reduce-scatter.4
  128.3 22.5 all-gather.6
  162.6 44.5 reduce-scatter.6
  215.3 22.5 all-gather.8
  250.0 44.5 reduce-scatter.8
  301.0 22.5 all-gather.10
  466.9 44.5 reduce-scatter.10
  516.8 395.6 all-reduce.3
where the time goes:
time: 941 us; the launch traced here: 931 us
  waiting for transfers between devices  604 us (64%)
  matrix products  162 us (17%)
  local copies, waits for them, and re-layouts  55 us (6%)
  blocking collectives  43.8 us (5%)
  other arithmetic  42.7 us (5%)
  between operations  14.8 us (2%)
    psum x1, waiting for transfers between devices, per_device(): lax.psum((grad_qkv, grad_wout, grad_up, grad_down), 'dp')  353 us
    reduce_scatter x4, waiting for transfers between devices, row_sums(): lax.psum_scatter(term(jnp.int32(0), own_rows * lax.axis_size('tensor')),...  161 us
    all_gather x4, waiting for transfers between devices, gather_rows(): return lax.all_gather(values_in, 'tensor', axis=0, tiled=True)  89.1 us
    dot_general x2, matrix products, step_back(): jnp.einsum('hqk,qhd->khd', grad_scores, query_block, preferred_element_ty...  46.3 us
    psum x1, blocking collectives, per_device(): lax.psum((jnp.stack([gain0, gain1, gain2, gain3], axis=0), jnp.stack([bia...  43.8 us
    dot_general x2, matrix products, step_back(): jnp.einsum('hqk,khd->qhd', grad_scores, key_rot, preferred_element_type=j...  34.3 us
    dynamic_update_slice x4, local copies, waits for them, and re-layouts, attention_backward(): lax.scan(step_back, (zeros_kv, zeros_kv), (offsets, log_total))  21.7 us
  transfers between devices with their start and end apart: 9, of which 9 were waited for; matrix products, arithmetic and copies ran while one was open for 3% of the time, Pallas kernels for 0%

commit v1 on v0

--- a/solution.py
+++ b/solution.py
@@ -1,3 +1,4 @@
+import functools
 import jax
 import jax.numpy as jnp
 from jax import lax
@@ -5,6 +6,37 @@
 
 HEAD_DIM = 64
 eps = 1e-05
+
+
+def lift_corner(raw, in_dim):
+    raw = jnp.moveaxis(raw, 0, in_dim)
+    kept_arr = raw.shape
+    return raw.reshape(
+        *kept_arr[:in_dim], kept_arr[in_dim] * kept_arr[in_dim + 1], *kept_arr[in_dim + 2 :]
+    )
+
+
+def _produce_spots(frame_in, link_axis):
+    total_devices = lax.psum(1, link_axis)
+    reached = frame_in[None]
+    for i0 in range(total_devices.bit_length() - 1):
+        current_block = 1 << i0
+        local_part = lax.ppermute(
+            reached,
+            link_axis,
+            perm=tuple(((num, num ^ current_block) for num in range(total_devices))),
+        )
+        a_now = jnp.stack([reached, local_part], axis=0)
+        state_now = lax.axis_index(link_axis) >> i0 & 1
+        reached = jnp.where(state_now == 0, a_now, a_now[::-1]).reshape(-1, *frame_in.shape)
+    return reached
+
+
+def _note_page(original, on_dim, mine):
+    return lift_corner(_produce_spots(original, mine), on_dim)
+
+
+spread_records = functools.partial(_note_page, on_dim=0, mine="tensor")
 
 
 def rope_tables(doc_row):
@@ -81,7 +113,7 @@
 
 
 def gather_rows(values_in):
-    return lax.all_gather(values_in, "tensor", axis=0, tiled=True)
+    return spread_records(values_in)
 
 
 def row_sums(term, own_rows):

time: 941 us -> 973 us (1.034)
  waiting for transfers between devices: 604 us -> 618 us
    ppermute x0 -> x8, waiting for transfers between devices: none -> 102 us  [_produce_spots(): lax.ppermute(reached, link_axis, perm=tuple(((num, num ^ current_block) f...]
    all_gather x4 -> x0, waiting for transfers between devices: 89.1 us -> none  [gather_rows(): return lax.all_gather(values_in, 'tensor', axis=0, tiled=True)]
    unnamed x79 -> x99, local copies, waits for them, and re-layouts: 18.3 us -> 22.5 us
  transfers between devices with their start and end apart: 9 -> 13, of which waited for: 9 -> 13; matrix products, arithmetic and copies ran while one was open for 3% -> 2% of each run, Pallas kernels for 0% -> 0%
where the time goes in v1:
time: 973 us; the launch traced here: 963 us
  waiting for transfers between devices  618 us (64%)
  matrix products  154 us (16%)
  local copies, waits for them, and re-layouts  58.9 us (6%)
  other arithmetic  50.7 us (5%)
  blocking collectives  43.6 us (4%)
  loops' own time  17.9 us (2%)
  between operations  14.9 us (2%)
    psum x1, waiting for transfers between devices, per_device(): lax.psum((grad_qkv, grad_wout, grad_up, grad_down), 'dp')  353 us
    reduce_scatter x4, waiting for transfers between devices, row_sums(): lax.psum_scatter(term(jnp.int32(0), own_rows * lax.axis_size('tensor')),...  163 us
    ppermute x8, waiting for transfers between devices, _produce_spots(): lax.ppermute(reached, link_axis, perm=tuple(((num, num ^ current_block) f...  102 us
    dot_general x2, matrix products, step_back(): jnp.einsum('hqk,qhd->khd', grad_scores, query_block, preferred_element_ty...  46.3 us
    psum x1, blocking collectives, per_device(): lax.psum((jnp.stack([gain0, gain1, gain2, gain3], axis=0), jnp.stack([bia...  43.6 us
    dot_general x2, matrix products, step_back(): jnp.einsum('hqk,khd->qhd', grad_scores, key_rot, preferred_element_type=j...  34.3 us
    unnamed x99, local copies, waits for them, and re-layouts  22.5 us
    dynamic_update_slice x4, local copies, waits for them, and re-layouts, attention_backward(): lax.scan(step_back, (zeros_kv, zeros_kv), (offsets, log_total))  21.7 us
  transfers between devices with their start and end apart: 13, of which 13 were waited for; matrix products, arithmetic and copies ran while one was open for 2% of the time, Pallas kernels for 0%

profile of v1, /device:TPU:0, one launch (start us, length us, event | category | flops | bytes accessed | tf_op | source)
XLA Modules:
  0.0 963.1 jit_solution(10013970504653819965)
XLA Ops:
  23.4 21.4 %collective-permute-done.1 = bf16[2,256,1024]{2,1,0:T(8,128)(2,1)} collective-permute-done((bf16[2,256,1024]{2,1,0:T(8,128)(2,1)}, bf16[2,256,1024]{2,1,0:T(8,128)(2,1)}, u32[]{:S(2)}, u32[]{:S(2)}) %collective-permute-start.1) | collective-permute-done | bytes 1048608 | tf_op jit(solution)/shard_map/ppermute | solution.py:24
  50.6 25.8 %while.27 = (s32[]{:T(128)}, bf16[2,512,4,64]{1,3,2,0:T(8,128)(2,1)}, f32[2,4,512]{2,1,0:T(4,128)S(1)}, s32[2]{0:T(128)S(1)}, s32[1,1024]{1,0:T(1,128)S(1)}, /*i...) while((s32[]{:T(128)}, ...), condition=%wide.region_7.8_spmd, body=%wide.region_4.7_spmd.sunk | while | flops 563739136 | bytes 33110264 | solution.py:150
  59.7 3.0 fusion.194
  78.9 3.8 fusion.130
  83.0 45.9 %reduce-scatter.5.cloned.1.call-done = f32[256,1024]{1,0:T(8,128)} async-done(((f32[1024,1024]{1,0:T(8,128)}), f32[256,1024]{1,0:T(8,128)}) %reduce-scatter.5.cloned.1.call-update) | async-done | bytes 1048592 | tf_op jit(solution)/shard_map/reduce_scatter | solution.py:120
  136.8 24.9 %collective-permute-done.3 = bf16[2,256,1024]{2,1,0:T(8,128)(2,1)S(1)} collective-permute-done((bf16[2,256,1024]{2,1,0:T(8,128)(2,1)S(1)}, bf16[2,256,1024]{2,1,0:T(8,128)(2,1)S(1)}, u32[]{:S(2)}, u32[]{:S(2)}) %collective-permute-start.3) | collective-permute-done | bytes 1048608 | tf_op jit(solution)/shard_map/ppermute | solution.py:24
  162.5 4.1 multiply_convert_fusion.1
  167.9 4.3 fusion.131
  172.4 44.7 %reduce-scatter.7.cloned.1.call-done = f32[256,1024]{1,0:T(8,128)} async-done(((f32[1024,1024]{1,0:T(8,128)}), f32[256,1024]{1,0:T(8,128)}) %reduce-scatter.7.cloned.1.call-update) | async-done | bytes 1048592 | tf_op jit(solution)/shard_map/reduce_scatter | solution.py:120
  228.1 24.9 %collective-permute-done.5 = bf16[2,256,1024]{2,1,0:T(8,128)(2,1)S(1)} collective-permute-done((bf16[2,256,1024]{2,1,0:T(8,128)(2,1)S(1)}, bf16[2,256,1024]{2,1,0:T(8,128)(2,1)S(1)}, u32[]{:S(2)}, u32[]{:S(2)}) %collective-permute-start.5) | collective-permute-done | bytes 1048608 | tf_op jit(solution)/shard_map/ppermute | solution.py:24
  256.5 3.6 fusion.85
  261.5 4.5 fusion.132
  266.0 44.7 %reduce-scatter.9.cloned.1.call-done = f32[256,1024]{1,0:T(8,128)} async-done(((f32[1024,1024]{1,0:T(8,128)}), f32[256,1024]{1,0:T(8,128)}) %reduce-scatter.9.cloned.1.call-update) | async-done | bytes 1048592 | tf_op jit(solution)/shard_map/reduce_scatter | solution.py:120
  318.1 25.0 %collective-permute-done.7 = bf16[2,256,1024]{2,1,0:T(8,128)(2,1)} collective-permute-done((bf16[2,256,1024]{2,1,0:T(8,128)(2,1)S(1)}, bf16[2,256,1024]{2,1,0:T(8,128)(2,1)}, u32[]{:S(2)}, u32[]{:S(2)}) %collective-permute-start.7) | collective-permute-done | bytes 1048608 | tf_op jit(solution)/shard_map/ppermute | solution.py:24
  347.2 140.6 %while.28 = (s32[]{:T(128)}, f32[1024,4,64]{0,2,1:T(8,128)}, f32[1024,4,64]{0,2,1:T(8,128)}, f32[2,512,4,64]{1,0,3,2:T(2,128)}, s32[2]{0:T(128)S(1)}, /*index=5*...) while((s32[]{:T(128)}, f32[1024,4,64]{0,2,1:T(8,128)}, ...), condition=%wide.region_25.26_spmd.clone, body=%wide.region_23.25_spmd.clone.sunk | while | flops 1399331328 | bytes 129562944 | solution.py:190
  366.4 4.6 fusion.205
  371.0 17.1 %fusion.210 = f32[1,512,4,64]{1,3,2,0:T(8,128)S(1)} fusion(bf16[1024,4,64]{0,2,1:T(8,128)(2,1)S(1)} %get-tuple-element.495, f32[4,512,1024]{2,1,0:T(8,128)} %fusion.205, f32[4,512,1024]{2,1,0:T(8,128)} %copy-done.2, f32[4,512]{1,0:T(4,128)S(1)} %dynamic-slice_bitcast_fusion.2, pred[512,1024]{1,0:T(8,128)(4,1)S(1)} %fusion.207), kind=kOutput, calls=%fused_computation.42.clone.1 | convolution fusion | flops 291507200 | bytes 18358272 | tf_op jit(solution)/shard_map/while/body/eval_jaxpr/hqk,khd->qhd/dot_general | solution.py:174
  388.2 23.1 %fusion.208 = f32[1024,4,64]{0,2,1:T(8,128)} fusion(f32[4,512,1024]{2,1,0:T(8,128)} %fusion.205, f32[4,512,1024]{2,1,0:T(8,128)} %copy-done.2, f32[4,512]{1,0:T(4,128)S(1)} %dynamic-slice_bitcast_fusion.2, pred[512,1024]{1,0:T(8,128)(4,1)S(1)} %fusion.207, f32[1024,4,64]{0,2,1:T(8,128)} %get-tuple-element.473, pred[]{:T(512)S(6)} %compare.3, ...), kind=kOutput, calls=%fused_computation.40.clone.1 | convolution fusion | flops 292031488 | bytes 36978692 | tf_op jit(solution)/shard_map/while/body/eval_jaxpr/hqk,qhd->khd/dot_general | solution.py:177
  411.9 10.3 %dynamic_update_slice.20 = f32[2,512,4,64]{1,0,3,2:T(2,128)} dynamic-update-slice(f32[2,512,4,64]{1,0,3,2:T(2,128)} %get-tuple-element.475, f32[1,512,4,64]{1,0,3,2:T(1,128)S(1)} %copy.65, s32[]{:T(128)S(6)} %copy.82, s32[]{:T(128)} %constant.80.clone.1..sunk.1, s32[]{:T(128)} %constant.80.clone.1..sunk.1, s32[]{:T(128)} %constant.80.clone.1..sunk.1) | dynamic-update-slice | bytes 1048580 | tf_op jit(solution)/shard_map/while/body/jit(dynamic_update_index_in_dim)/dynamic_update_slice | solution.py:190
  431.9 4.6 fusion.205
  436.5 17.1 %fusion.210 = f32[1,512,4,64]{1,3,2,0:T(8,128)S(1)} fusion(bf16[1024,4,64]{0,2,1:T(8,128)(2,1)S(1)} %get-tuple-element.495, f32[4,512,1024]{2,1,0:T(8,128)} %fusion.205, f32[4,512,1024]{2,1,0:T(8,128)} %copy-done.2, f32[4,512]{1,0:T(4,128)S(1)} %dynamic-slice_bitcast_fusion.2, pred[512,1024]{1,0:T(8,128)(4,1)S(1)} %fusion.207), kind=kOutput, calls=%fused_computation.42.clone.1 | convolution fusion | flops 291507200 | bytes 18358272 | tf_op jit(solution)/shard_map/while/body/eval_jaxpr/hqk,khd->qhd/dot_general | solution.py:174
  453.6 23.2 %fusion.208 = f32[1024,4,64]{0,2,1:T(8,128)} fusion(f32[4,512,1024]{2,1,0:T(8,128)} %fusion.205, f32[4,512,1024]{2,1,0:T(8,128)} %copy-done.2, f32[4,512]{1,0:T(4,128)S(1)} %dynamic-slice_bitcast_fusion.2, pred[512,1024]{1,0:T(8,128)(4,1)S(1)} %fusion.207, f32[1024,4,64]{0,2,1:T(8,128)} %get-tuple-element.473, pred[]{:T(512)S(6)} %compare.3, ...), kind=kOutput, calls=%fused_computation.40.clone.1 | convolution fusion | flops 292031488 | bytes 36978692 | tf_op jit(solution)/shard_map/while/body/eval_jaxpr/hqk,qhd->khd/dot_general | solution.py:177
  477.3 10.3 %dynamic_update_slice.20 = f32[2,512,4,64]{1,0,3,2:T(2,128)} dynamic-update-slice(f32[2,512,4,64]{1,0,3,2:T(2,128)} %get-tuple-element.475, f32[1,512,4,64]{1,0,3,2:T(1,128)S(1)} %copy.65, s32[]{:T(128)S(6)} %copy.82, s32[]{:T(128)} %constant.80.clone.1..sunk.1, s32[]{:T(128)} %constant.80.clone.1..sunk.1, s32[]{:T(128)} %constant.80.clone.1..sunk.1) | dynamic-update-slice | bytes 1048580 | tf_op jit(solution)/shard_map/while/body/jit(dynamic_update_index_in_dim)/dynamic_update_slice | solution.py:190
  493.7 5.2 convolution_bitcast_fusion
  500.5 6.1 fusion.135
  506.6 4.4 fusion.134
  512.8 3.5 convolution_bitcast_fusion.1
  516.4 27.3 %reduce-scatter.11.cloned.1.call-done = f32[256,1024]{1,0:T(8,128)} async-done(((f32[1024,1024]{1,0:T(8,128)}), f32[256,1024]{1,0:T(8,128)}) %reduce-scatter.11.cloned.1.call-update) | async-done | bytes 1048592 | tf_op jit(solution)/shard_map/reduce_scatter | solution.py:120
  545.6 43.6 %all-reduce = (f32[4,1024]{1,0:T(4,128)}, f32[4,1024]{1,0:T(4,128)}) all-reduce(f32[4,1024]{1,0:T(4,128)S(1)} %pad_maximum_fusion.15, f32[4,1024]{1,0:T(4,128)S(1)} %pad_maximum_fusion.16), channel_id=1, replica_groups=mesh['dp'=8,'tensor'=4] {'dp','tensor'}, use_global_device_ids=true, to_apply=%region_37.38 | all-reduce | flops 8192 | bytes 65536 | tf_op jit(solution)/shard_map/psum | solution.py:280
  591.6 353.0 %all-reduce.4.cloned.1.call-done = (f32[3,1024,256]{1,2,0:T(8,128)}, f32[256,1024]{1,0:T(8,128)}, f32[1024,1024]{1,0:T(8,128)}, f32[1024,1024]{1,0:T(8,128)}) async-done(((f32[3,1024,256]{1,2,0:T(8,128)}, f32[256,1024]{1,0:T(8,128)}, f32[1024,1024]{1,0:T(8,128)}, f32[1024,1024]{1,0:T(8,128)}), (f32[3,1024,256]{1,2,0:T(8,128)}, f32[256,1024]{1,0:T(8,128)}, f32[1024,1024]{1,0:T(8,128)}, ...) | async-done | bytes 12582928 | tf_op jit(solution)/shard_map/psum | solution.py:277
  944.6 3.6 copy.34
  949.2 4.9 copy.95
  (256 shorter events, 113.5 us)
Async XLA Ops:
  7.2 155.3 %copy-start = (bf16[1024,1024]{1,0:T(8,128)(2,1)S(1)}, bf16[1024,1024]{1,0:T(8,128)(2,1)}, u32[]{:S(2)}) copy-start(bf16[1024,1024]{1,0:T(8,128)(2,1)} %param.17) | copy-start | bytes 6291460
  7.2 13.8 %copy-start.21 = (s32[1,1024]{1,0:T(1,128)S(1)}, s32[1,1024]{1,0:T(1,128)}, u32[]{:S(2)}) copy-start(s32[1,1024]{1,0:T(1,128)} %param.14) | copy-start | bytes 12292
  7.2 121.7 %reduce-scatter.5.cloned.1.call-start = ((), (), s32[]{:S(2)}) async-start(), calls=%async_computation.4 | async-start | bytes 5242880 | tf_op jit(solution)/shard_map/reduce_scatter | solution.py:120
  8.6 12.9 %copy-start.39 = (f32[256]{0:T(256)}, f32[256]{0:T(256)S(1)}, u32[]{:S(2)}) copy-start(f32[256]{0:T(256)S(1)} %broadcast_multiply_fusion.11) | copy-start | bytes 3076
  9.9 36.7 %copy-start.41 = (f32[256]{0:T(256)}, f32[256]{0:T(256)S(1)}, u32[]{:S(2)}) copy-start(f32[256]{0:T(256)S(1)} %add_rsqrt_fusion.3) | copy-start | bytes 3076
  13.0 2.2 collective-permute-start
  18.1 26.6 %collective-permute-start.1 = (bf16[2,256,1024]{2,1,0:T(8,128)(2,1)}, bf16[2,256,1024]{2,1,0:T(8,128)(2,1)}, u32[]{:S(2)}, u32[]{:S(2)}) collective-permute-start(bf16[2,256,1024]{2,1,0:T(8,128)(2,1)} %get-tuple-element.268), channel_id=1, source_target_pairs={{0,2},{1,3},{2,0},{3,1},{4,6},{5,7},{6,4},{7,5},{8,10},{9,11},{10,... | collective-permute-start | bytes 3145736 | tf_op jit(solution)/shard_map/ppermute | solution.py:24
  23.4 26.0 %copy-start.22 = (f32[1024,32]{0,1:T(8,128)}, f32[1024,32]{0,1:T(8,128)S(1)}, u32[]{:S(2)}) copy-start(f32[1024,32]{0,1:T(8,128)S(1)} %get-tuple-element.283) | copy-start | bytes 393220
  23.4 26.0 %copy-start.24 = (f32[1024,32]{0,1:T(8,128)}, f32[1024,32]{0,1:T(8,128)S(1)}, u32[]{:S(2)}) copy-start(f32[1024,32]{0,1:T(8,128)S(1)} %get-tuple-element.284) | copy-start | bytes 393220
  82.7 134.3 %reduce-scatter.7.cloned.1.call-start = ((), (), s32[]{:S(2)}) async-start(), calls=%async_computation.5 | async-start | bytes 5242880 | tf_op jit(solution)/shard_map/reduce_scatter | solution.py:120
  134.1 2.0 collective-permute-start.2
  136.4 25.3 %collective-permute-start.3 = (bf16[2,256,1024]{2,1,0:T(8,128)(2,1)S(1)}, bf16[2,256,1024]{2,1,0:T(8,128)(2,1)S(1)}, u32[]{:S(2)}, u32[]{:S(2)}) collective-permute-start(bf16[2,256,1024]{2,1,0:T(8,128)(2,1)S(1)} %get-tuple-element.266), channel_id=1, source_target_pairs={{0,2},{1,3},{2,0},{3,1},{4,6},{5,7},{6,4},{7,5},{8,10},{9,11},{10,... | collective-permute-start | bytes 3145736 | tf_op jit(solution)/shard_map/ppermute | solution.py:24
  172.3 138.4 %reduce-scatter.9.cloned.1.call-start = ((), (), s32[]{:S(2)}) async-start(), calls=%async_computation.6 | async-start | bytes 5242880 | tf_op jit(solution)/shard_map/reduce_scatter | solution.py:120
  225.4 1.9 collective-permute-start.4
  227.6 25.3 %collective-permute-start.5 = (bf16[2,256,1024]{2,1,0:T(8,128)(2,1)S(1)}, bf16[2,256,1024]{2,1,0:T(8,128)(2,1)S(1)}, u32[]{:S(2)}, u32[]{:S(2)}) collective-permute-start(bf16[2,256,1024]{2,1,0:T(8,128)(2,1)S(1)} %get-tuple-element.264), channel_id=1, source_target_pairs={{0,2},{1,3},{2,0},{3,1},{4,6},{5,7},{6,4},{7,5},{8,10},{9,11},{10,... | collective-permute-start | bytes 3145736 | tf_op jit(solution)/shard_map/ppermute | solution.py:24
  253.7 6.4 copy-start.19
  265.9 44.8 %copy-start.4 = (f32[256,1024]{1,0:T(8,128)S(1)}, f32[256,1024]{1,0:T(8,128)}, u32[]{:S(2)}) copy-start(f32[256,1024]{1,0:T(8,128)} %copy-done.3) | copy-start | bytes 3145732
  265.9 46.5 %copy-start.5 = (f32[256,1024]{1,0:T(8,128)S(1)}, f32[256,1024]{1,0:T(8,128)}, u32[]{:S(2)}) copy-start(f32[256,1024]{1,0:T(8,128)} %reduce-scatter.5.cloned.1.call-done) | copy-start | bytes 3145732
  265.9 277.8 %reduce-scatter.11.cloned.1.call-start = ((), (), s32[]{:S(2)}) async-start(), calls=%async_computation.7 | async-start | bytes 5242880 | tf_op jit(solution)/shard_map/reduce_scatter | solution.py:120
  315.2 2.0 collective-permute-start.6
  317.6 25.4 %collective-permute-start.7 = (bf16[2,256,1024]{2,1,0:T(8,128)(2,1)S(1)}, bf16[2,256,1024]{2,1,0:T(8,128)(2,1)}, u32[]{:S(2)}, u32[]{:S(2)}) collective-permute-start(bf16[2,256,1024]{2,1,0:T(8,128)(2,1)S(1)} %get-tuple-element.262), channel_id=1, source_target_pairs={{0,2},{1,3},{2,0},{3,1},{4,6},{5,7},{6,4},{7,5},{8,10},{9,11},{10,... | collective-permute-start | bytes 3145736 | tf_op jit(solution)/shard_map/ppermute | solution.py:24
  347.2 142.8 %copy-start.23 = (f32[1024,32]{0,1:T(8,128)S(1)}, f32[1024,32]{0,1:T(8,128)}, u32[]{:S(2)}) copy-start(f32[1024,32]{0,1:T(8,128)} %copy-done.22) | copy-start | bytes 393220
  347.2 142.8 %copy-start.25 = (f32[1024,32]{0,1:T(8,128)S(1)}, f32[1024,32]{0,1:T(8,128)}, u32[]{:S(2)}) copy-start(f32[1024,32]{0,1:T(8,128)} %copy-done.24) | copy-start | bytes 393220
  499.0 445.6 %all-reduce.4.cloned.1.call-start = ((), (), s32[]{:S(2)}) async-start(), calls=%async_computation.8 | async-start | bytes 25165824 | tf_op jit(solution)/shard_map/psum | solution.py:277
  516.3 27.4 %copy-start.7 = (bf16[256,1024]{1,0:T(8,128)(2,1)S(1)}, bf16[256,1024]{1,0:T(8,128)(2,1)}, u32[]{:S(2)}) copy-start(bf16[256,1024]{1,0:T(8,128)(2,1)} %param.13) | copy-start | bytes 1572868
  516.3 27.4 %copy-start.38 = (f32[1,1024]{1,0:T(1,128)S(1)}, f32[1,1024]{1,0:T(1,128)}, u32[]{:S(2)}) copy-start(f32[1,1024]{1,0:T(1,128)} %copy-done.37) | copy-start | bytes 12292
  516.3 27.4 %copy-start.40 = (f32[256]{0:T(256)S(1)}, f32[256]{0:T(256)}, u32[]{:S(2)}) copy-start(f32[256]{0:T(256)} %copy-done.39) | copy-start | bytes 3076
  516.3 27.4 %copy-start.42 = (f32[256]{0:T(256)S(1)}, f32[256]{0:T(256)}, u32[]{:S(2)}) copy-start(f32[256]{0:T(256)} %copy-done.41) | copy-start | bytes 3076
  516.3 29.2 %copy-start.44 = (f32[1024]{0:T(1024)S(1)}, f32[1024]{0:T(1024)}, u32[]{:S(2)}) copy-start(f32[1024]{0:T(1024)} %get-tuple-element.186) | copy-start | bytes 12292
  516.4 29.2 %copy-start.43 = (f32[1024]{0:T(1024)S(1)}, f32[1024]{0:T(1024)}, u32[]{:S(2)}) copy-start(f32[1024]{0:T(1024)} %get-tuple-element.195) | copy-start | bytes 12292
  516.4 72.8 %copy-start.9 = (f32[256,1024]{1,0:T(8,128)S(1)}, f32[256,1024]{1,0:T(8,128)}, u32[]{:S(2)}) copy-start(f32[256,1024]{1,0:T(8,128)} %copy-done.8) | copy-start | bytes 3145732
  949.2 7.0 copy-start.1
  (38 other events, 107.9 us)
Sparse Core Ops, SparseCore 0:
  82.8 46.0 reduce-scatter.4
  172.4 44.5 reduce-scatter.6
  266.1 44.5 reduce-scatter.8
  499.1 44.5 reduce-scatter.10
  548.9 395.6 all-reduce.3
